TPU v7x, 32 devices: a whole 2x2x4 slice. The times are simulated.
32 devices in a mesh: groups: 2 (over y), space: 4 (over z), date: 2 (over x), band: 2 (over core).
Axes of the slice: x: 2, y: 2, z: 4, core: 2. Of those that a mesh axis runs over, the one named last changes fastest.
Arguments:
- reflect: float32 [16, 8, 256, 256], P('date', 'band', ('groups', 'space')), parts along dimension 2, may hold values from -6 to 6
- kernels: float32 [3, 8, 33], P(None, 'band'), may hold values from 0.2 to 2
- strength: float32 [3, 8], P(None, 'band'), may hold values from 0.2 to 0.6
- destinations: int32 [128, 1], P(('groups', 'space')), parts along dimension 0, may hold values from 0 to 3; in each aligned block of 16 rows (0 to 15, 16 to 31, ...) at most 8 rows name the same one
- offsets: int32 [128], P(('groups', 'space')), parts along dimension 0, may hold values from 0 to 60
- counts: int32 [16, 8], P('date', ('groups', 'space')), parts along dimension 1, may hold values from 1 to 8192
- resample_rows: float32 [8, 4, 4], P(('groups', 'space')), parts along dimension 0, may hold values from -3 to 3
- resample_columns: float32 [8, 128, 128], P(('groups', 'space')), parts along dimension 0, may hold values from -0.5 to 0.5
Outputs:
- geomedian: float32 [8, 512, 128], P('band', ('groups', 'space')), parts along dimension 1
There are 2 independent parts, one for each index of `groups`. A program takes and returns all parts, laid end to end along the dimension named above; an argument that names none is the same for every part. Nothing has to cross between parts.
Inputs may be any that keep to these rules, and one draw needn't show every extreme that they name: `destinations`: in each aligned block of 16 entries (the blocks of one strip) no tile is named more than 8 times, a bound that some block reaches.
All inputs are finite; a program needn't handle non-finite values.
Results may differ from a plain program's by a relative error of at most 0.00011.
Values sent between devices are 32-bit elements; how exact they have to be, the bound alone decides.
No kernel may reach another device: no remote copies, remote signals or barrier semaphores. Data moves between devices by JAX's collectives and lax.ppermute only.
A program may use at most 128 MiB of HBM per device.

v0:
```python
import jax
import jax.numpy as jnp
from jax import lax
from jax.sharding import PartitionSpec as P

BROWS = 4
BCOLS = 128
ITERS = 4


highest = lax.Precision.HIGHEST
smooth_sq = 0.01


def padded_2(block, sides, width):
    for axis, dim in sides:
        count = lax.axis_size(axis)
        forward = [(i, i + 1) for i in range(count - 1)]
        backward = [(target, source) for source, target in forward]
        low = lax.ppermute(
            lax.slice_in_dim(block, block.shape[dim] - width, None, axis=dim), axis, forward
        )
        high = lax.ppermute(lax.slice_in_dim(block, 0, width, axis=dim), axis, backward)
        block = jnp.concatenate([low, block, high], axis=dim)
    return block


def band_matrix(weights, count_out, count_in, lead_shift):
    tap_count = weights.shape[1]
    offset = jnp.arange(count_in)[None, :] - jnp.arange(count_out)[:, None] + lead_shift
    matrix = jnp.zeros((weights.shape[0], count_out, count_in), jnp.float32)
    for tap_index in range(tap_count):
        chosen = (offset == tap_index).astype(jnp.float32)
        matrix = matrix + weights[:, tap_index, None, None] * chosen[None, :, :]
    return matrix


def correct_strip(values, kernels, strength):
    radius = (kernels.shape[2] - 1) // 2
    strip_rows = values.shape[2]
    column_count = values.shape[3]
    for pass_index in range(kernels.shape[0]):
        norm_taps = kernels[pass_index] / jnp.sum(kernels[pass_index], axis=1, keepdims=True)
        row_matrix = band_matrix(norm_taps, strip_rows, strip_rows + 2 * radius, 0)
        column_matrix = band_matrix(norm_taps, column_count, column_count, radius)
        padded = padded_2(values, (("space", 2),), radius)
        row_pass = jnp.einsum("bij,tbjc->tbic", row_matrix, padded, precision=highest)
        blurred = jnp.einsum("tbrj,bcj->tbrc", row_pass, column_matrix, precision=highest)
        values = values + strength[pass_index][None, :, None, None] * (values - blurred)
    return values


def cut_blocks(values):
    date_here, band_here, strip_rows, column_count = values.shape
    shaped = values.reshape(
        date_here, band_here, strip_rows // BROWS, BROWS, column_count // BCOLS, BCOLS
    )
    return shaped.transpose(2, 4, 0, 1, 3, 5).reshape(-1, date_here, band_here, BROWS, BCOLS)


def pack_slots(blocks, targets, starts, tile_count, capacity):
    onehot = (targets[:, None] == jnp.arange(tile_count)[None, :]).astype(jnp.int32)
    before = jnp.cumsum(onehot, axis=0) - onehot
    ranked = jnp.sum(before * onehot, axis=1)
    slot_index = targets * capacity + ranked
    placer = (slot_index[None, :] == jnp.arange(tile_count * capacity)[:, None]).astype(jnp.float32)
    packed = jnp.einsum("sn,ntbrc->stbrc", placer, blocks, precision=highest)
    moved_starts = jnp.dot(placer, starts.astype(jnp.float32), precision=highest)
    shape_out = (tile_count, capacity) + blocks.shape[1:]
    return (packed.reshape(shape_out), moved_starts.reshape(tile_count, capacity))


def lay_tile(slot_data, slot_starts, tile_rows):
    flat_rows = slot_data.reshape((-1,) + slot_data.shape[2:])
    first_row = slot_starts.reshape(-1).astype(jnp.int32)
    target_row = first_row[:, None] + jnp.arange(BROWS, dtype=jnp.int32)[None, :]
    placer = (
        target_row[:, :, None] == jnp.arange(tile_rows, dtype=jnp.int32)[None, None, :]
    ).astype(jnp.float32)
    return jnp.einsum("sij,stbic->tbjc", placer, flat_rows, precision=highest)


def band_total(squares):
    return lax.psum(squares, "band")


def keep_local(numerator, denominator):
    return (numerator, denominator)


def geomedian_steps(stacked, weight_column, combine):
    numerator = jnp.sum(weight_column[:, :, None] * stacked, axis=0)
    denominator = jnp.sum(weight_column) * jnp.ones((stacked.shape[2],), jnp.float32)
    numerator, denominator = combine(numerator, denominator)
    estimate = numerator / denominator[None, :]
    for iter_index in range(ITERS):
        partial_sq = jnp.sum((stacked - estimate[None]) ** 2, axis=1)
        distance = jnp.sqrt(band_total(partial_sq) + smooth_sq)
        scaled = weight_column / distance
        numerator = jnp.sum(scaled[:, None, :] * stacked, axis=0)
        denominator = jnp.sum(scaled, axis=0)
        numerator, denominator = combine(numerator, denominator)
        estimate = numerator / denominator[None, :]
    return estimate


def local(
    reflect, kernels, strength, destinations, offsets, counts, resample_rows, resample_columns
):
    corrected = correct_strip(reflect, kernels, strength)
    blocks = cut_blocks(corrected)
    tile_count = lax.axis_size("space")
    block_count = blocks.shape[0]
    capacity = max(2, 2 * block_count // tile_count)
    targets = destinations[:, 0]
    count_here = counts.astype(jnp.float32)
    count_part = jnp.sum(count_here)
    packed, starts = pack_slots(blocks, targets, offsets, tile_count, capacity)
    own_rows = resample_rows[0]
    own_columns = resample_columns[0]
    raw_blocks = lax.all_to_all(packed, "space", split_axis=0, concat_axis=0, tiled=True)
    raw_starts = lax.all_to_all(starts, "space", split_axis=0, concat_axis=0, tiled=True)
    row_pass = jnp.einsum("ij,smtbjc->smtbic", own_rows, raw_blocks, precision=highest)
    final_blocks = jnp.einsum("smtbic,cv->smtbiv", row_pass, own_columns, precision=highest)
    tile_rows = block_count * BROWS
    assembled = lay_tile(final_blocks, raw_starts, tile_rows)
    count_sum = lax.psum(count_part, ("space", "date"))
    mean_count = count_sum / (counts.shape[0] * lax.axis_size("date") * tile_count)
    weight_column = count_here / (count_here + mean_count)
    date_here = assembled.shape[0]
    band_here = assembled.shape[1]
    pixels = tile_rows * BCOLS
    stacked = assembled.reshape(date_here, band_here, pixels)
    date_count = lax.axis_size("date")
    spread = jnp.broadcast_to(weight_column[:, :, None], (date_here, 1, date_count))
    whole_stack, whole_weight = (
        lax.all_to_all(stacked, "date", split_axis=2, concat_axis=0, tiled=True),
        lax.all_to_all(spread, "date", split_axis=2, concat_axis=0, tiled=True),
    )
    part_estimate = geomedian_steps(whole_stack, whole_weight.reshape(-1, 1), keep_local)
    estimate = lax.all_gather(part_estimate, "date", axis=1, tiled=True)
    return estimate.reshape(band_here, tile_rows, BCOLS)


def solution(mesh):
    in_specs = (
        P("date", "band", ("groups", "space"), None),
        P(None, "band", None),
        P(None, "band"),
        P(("groups", "space"), None),
        P(("groups", "space")),
        P("date", ("groups", "space")),
        P(("groups", "space"), None, None),
        P(("groups", "space"), None, None),
    )
    out_specs = P("band", ("groups", "space"), None)
    return jax.shard_map(local, mesh=mesh, in_specs=in_specs, out_specs=out_specs, check_vma=False)
```

profile of v0, /device:TPU:0, one launch (start us, length us, event | category | flops | bytes accessed | tf_op | source)
XLA Modules:
  0.0 362.7 jit_solution(205824982258235343)
XLA Ops:
  6.5 1.3 fusion.1005
  7.9 5.0 %collective-permute-start = (f32[8,4,16,256]{3,2,0,1:T(8,128)S(1)}, f32[8,4,16,256]{3,2,0,1:T(8,128)S(1)}, u32[]{:S(2)}, u32[]{:S(2)}) collective-permute-start(f32[8,4,16,256]{3,2,0,1:T(8,128)S(1)} %get-tuple-element.111), channel_id=1, source_target_pairs={{0,4},{4,8},{8,12},{1,5},{5,9},{9,13},{2,6},{6,10},{10,14},{3,7},{... | collective-permute-start | bytes 1572872 | tf_op jit(solution)/shard_map/ppermute | solution.py:20
  12.9 1.3 collective-permute-start.1
  24.4 3.7 %collective-permute-done.1 = f32[8,4,16,256]{3,2,0,1:T(8,128)S(1)} collective-permute-done((f32[8,4,16,256]{3,2,0,1:T(8,128)S(1)}, f32[8,4,16,256]{3,2,0,1:T(8,128)S(1)}, u32[]{:S(2)}, u32[]{:S(2)}) %collective-permute-start.1) | collective-permute-done | bytes 524320 | tf_op jit(solution)/shard_map/ppermute | solution.py:23
  28.2 2.6 fusion.28
  31.1 4.4 %fusion.39 = f32[8,4,32,256]{3,2,0,1:T(8,128)S(1)} fusion(f32[8,4,32,256]{3,2,0,1:T(8,128)S(1)} %fusion.28, f32[256,256]{1,0:T(8,128)S(1)} %fusion.517, f32[4]{0:T(128)S(1)} %get-tuple-element.75, f32[256,256]{1,0:T(8,128)S(1)} %get-tuple-element.190, f32[4]{0:T(128)S(1)} %get-tuple-element.76, f32[256,256]{1,0:T(8,128)S(1)} %get-tuple-element.189, ...), kind=kOutput, calls=%fused_computation.37 | convolution fusion | flops 823132160 | bytes 11797024 | tf_op jit(solution)/shard_map/tbrj,bcj->tbrc/dot_general | solution.py:48
  35.6 4.3 %collective-permute-start.2 = (f32[8,4,16,256]{3,2,0,1:T(8,128)S(1)}, f32[8,4,16,256]{3,2,0,1:T(8,128)}, u32[]{:S(2)}, u32[]{:S(2)}) collective-permute-start(f32[8,4,16,256]{3,2,0,1:T(8,128)S(1)} %get-tuple-element.109), channel_id=1, source_target_pairs={{0,4},{4,8},{8,12},{1,5},{5,9},{9,13},{2,6},{6,10},{10,14},{3,7},{... | collective-permute-start | bytes 1572872 | tf_op jit(solution)/shard_map/ppermute | solution.py:20
  39.9 1.5 collective-permute-start.3
  42.7 6.4 %collective-permute-done.2 = f32[8,4,16,256]{3,2,0,1:T(8,128)} collective-permute-done((f32[8,4,16,256]{3,2,0,1:T(8,128)S(1)}, f32[8,4,16,256]{3,2,0,1:T(8,128)}, u32[]{:S(2)}, u32[]{:S(2)}) %collective-permute-start.2) | collective-permute-done | bytes 524320 | tf_op jit(solution)/shard_map/ppermute | solution.py:20
  49.1 5.0 %collective-permute-done.3 = f32[8,4,16,256]{3,2,0,1:T(8,128)} collective-permute-done((f32[8,4,16,256]{3,2,0,1:T(8,128)S(1)}, f32[8,4,16,256]{3,2,0,1:T(8,128)}, u32[]{:S(2)}, u32[]{:S(2)}) %collective-permute-start.3) | collective-permute-done | bytes 524320 | tf_op jit(solution)/shard_map/ppermute | solution.py:23
  54.1 2.8 fusion.25
  57.1 6.2 %fusion.36 = f32[8,4,32,256]{3,2,0,1:T(8,128)S(1)} fusion(f32[8,4,32,256]{3,2,0,1:T(8,128)S(1)} %fusion.39, f32[8,4,32,256]{3,2,0,1:T(8,128)S(1)} %fusion.25, f32[4]{0:T(128)S(1)} %get-tuple-element.42, f32[4]{0:T(128)S(1)} %get-tuple-element.43, f32[4]{0:T(128)S(1)} %get-tuple-element.44, f32[4]{0:T(128)S(1)} %get-tuple-element.45, ...), kind=kOutput, calls=%fused_computation.33 | convolution fusion | flops 823132160 | bytes 11797024 | tf_op jit(solution)/shard_map/tbrj,bcj->tbrc/dot_general | solution.py:48
  63.5 2.7 collective-permute-start.4
  66.2 1.3 collective-permute-start.5
  67.7 0.7 all_to_all.35
  68.4 4.2 %all-to-all-start.2 = ((f32[4,1,8]{2,1,0:T(1,128)}), f32[4,1,8]{2,1,0:T(1,128)S(1)}, u32[]{:S(2)}, u32[]{:S(2)}) async-start(f32[4,1,8]{2,1,0:T(1,128)} %bitcast.43), calls=%async_computation.2 | async-start | bytes 4096 | tf_op jit(solution)/shard_map/all_to_all | solution.py:122
  73.4 1.7 collective-permute-done.4
  75.1 4.3 %collective-permute-done.5 = f32[8,4,16,256]{3,2,0,1:T(8,128)} collective-permute-done((f32[8,4,16,256]{3,2,0,1:T(8,128)S(1)}, f32[8,4,16,256]{3,2,0,1:T(8,128)}, u32[]{:S(2)}, u32[]{:S(2)}) %collective-permute-start.5) | collective-permute-done | bytes 524320 | tf_op jit(solution)/shard_map/ppermute | solution.py:23
  79.4 2.7 fusion.22
  82.2 7.3 %fusion.33 = f32[8,4,32,256]{3,2,0,1:T(8,128)S(1)} fusion(f32[8,4,32,256]{3,2,0,1:T(8,128)S(1)} %fusion.36, f32[8,4,32,256]{3,2,0,1:T(8,128)S(1)} %fusion.22, f32[4]{0:T(128)S(1)} %get-tuple-element.9, f32[4]{0:T(128)S(1)} %get-tuple-element.10, f32[4]{0:T(128)S(1)} %get-tuple-element.11, f32[4]{0:T(128)S(1)} %get-tuple-element.12, ...), kind=kOutput, calls=%fused_computation.29 | convolution fusion | flops 823132160 | bytes 11797024 | tf_op jit(solution)/shard_map/tbrj,bcj->tbrc/dot_general | solution.py:48
  90.7 2.8 fusion.56
  93.5 3.7 %all-to-all-start.1 = ((f32[4,8,8,4,4,128]{5,1,4,3,2,0:T(8,128)}), f32[4,8,8,4,4,128]{5,1,4,3,2,0:T(8,128)S(1)}, u32[]{:S(2)}, u32[]{:S(2)}) async-start(f32[4,8,8,4,4,128]{5,1,4,3,2,0:T(8,128)} %fusion.56), calls=%async_computation.1 | async-start | bytes 4194304 | tf_op jit(solution)/shard_map/all_to_all | solution.py:121
  97.9 45.7 %psum.35 = f32[]{:T(128)} all-reduce(f32[]{:T(128)} %convert_reduce_fusion.1), channel_id=1, replica_groups=mesh['groups'=2,'space'=4,'date'=2,'band'=2] {'space','date'}, use_global_device_ids=true, to_apply=%region_1.0 | all-reduce | flops 1 | bytes 8 | tf_op jit(solution)/shard_map/psum | solution.py:127
  145.0 9.0 %all-to-all-start = ((f32[8,1,2]{0,1,2:T(1,128)}), f32[8,1,2]{0,1,2:T(1,128)S(1)}, u32[]{:S(2)}, u32[]{:S(2)}) async-start(f32[8,1,2]{0,1,2:T(1,128)} %broadcast_in_dim.5), calls=%async_computation | async-start | bytes 2048 | tf_op jit(solution)/shard_map/all_to_all | solution.py:138
  154.0 3.8 %fusion.20 = f32[4,8,8,4,128,4]{4,5,3,2,1,0:T(4,128)S(1)} fusion(f32[4,8,8,4,4,128]{5,1,4,3,2,0:T(8,128)S(1)} %all-to-all-done.1, f32[1,4,4]{2,1,0:T(4,128)S(1)} %copy-done.65), kind=kOutput, calls=%fused_computation.20 | convolution fusion | flops 25165824 | bytes 4194368 | tf_op jit(solution)/shard_map/ij,smtbjc->smtbic/dot_general | solution.py:123
  157.9 3.1 fusion.18
  161.0 1.0 convolution_bitcast_fusion
  162.0 8.6 %copy.90 = f32[8,4,64,128]{0,1,3,2:T(4,128)} copy(f32[8,4,64,128]{3,2,1,0:T(8,128)S(1)} %convolution_bitcast_fusion) | data formatting | bytes 2097152 | tf_op jit(solution)/shard_map/reshape | solution.py:133
  170.6 28.1 %reshape.1121 = f32[2,1,131072]{2,1,0:T(1,128)} reshape(f32[8192,4,8]{2,1,0:T(4,128)} %bitcast.199) | data formatting | bytes 2097152
  198.7 3.6 all-to-all-start.3
  203.2 9.7 %all-to-all-done.3 = f32[2,1,131072]{2,1,0:T(1,128)S(1)} async-done(((f32[2,1,131072]{2,1,0:T(1,128)}), f32[2,1,131072]{2,1,0:T(1,128)S(1)}, u32[]{:S(2)}, u32[]{:S(2)}) %all-to-all-start.3) | async-done | bytes 1048608 | tf_op jit(solution)/shard_map/all_to_all | solution.py:137
  213.5 4.0 %reduce.217 = f32[2,131072]{1,0:T(2,128)S(1)} reduce(f32[2,1,131072]{2,1,0:T(1,128)S(1)} %all-to-all-done.3, f32[]{:T(128)} %broadcast.1279), dimensions={1}, to_apply=%all_to_all.37.reduce_sub_computation | reduce | bytes 2097156 | tf_op jit(solution)/shard_map/all_to_all | solution.py:137
  217.5 26.1 %reshape.1122 = f32[8192,4,8]{2,1,0:T(4,128)} reshape(f32[2,131072]{1,0:T(2,128)S(1)} %reduce.217) | data formatting | bytes 2097152
  243.5 13.2 %copy.69 = f32[8,4,2,4096]{3,2,1,0:T(2,128)S(1)} copy(f32[8,4,2,4096]{0,1,3,2:T(4,128)} %bitcast.200) | data formatting | bytes 2097152 | tf_op jit(solution)/shard_map/all_to_all | solution.py:137
  258.0 0.7 fusion.45
  258.7 0.9 copy.114
  259.7 19.0 %all-reduce.5.cloned.1.call-done = f32[16,4096]{1,0:T(8,128)} async-done(((f32[16,4096]{1,0:T(8,128)}), f32[16,4096]{1,0:T(8,128)}) %all-reduce.5.cloned.1.call-update) | async-done | bytes 262160 | tf_op jit(solution)/shard_map/psum | solution.py:84
  278.7 1.1 fusion.518
  281.4 0.9 copy.113
  282.3 19.5 %all-reduce.7.cloned.1.call-done = f32[16,4096]{1,0:T(8,128)} async-done(((f32[16,4096]{1,0:T(8,128)}), f32[16,4096]{1,0:T(8,128)}) %all-reduce.7.cloned.1.call-update) | async-done | bytes 262160 | tf_op jit(solution)/shard_map/psum | solution.py:84
  301.8 1.1 fusion.520
  304.5 0.9 copy.112
  305.7 19.2 %all-reduce.9.cloned.1.call-done = f32[16,4096]{1,0:T(8,128)} async-done(((f32[16,4096]{1,0:T(8,128)}), f32[16,4096]{1,0:T(8,128)}) %all-reduce.9.cloned.1.call-update) | async-done | bytes 262160 | tf_op jit(solution)/shard_map/psum | solution.py:84
  325.0 1.1 fusion.522
  327.6 0.9 copy.111
  328.5 19.6 %all-reduce.11.cloned.1.call-done = f32[16,4096]{1,0:T(8,128)} async-done(((f32[16,4096]{1,0:T(8,128)}), f32[16,4096]{1,0:T(8,128)}) %all-reduce.11.cloned.1.call-update) | async-done | bytes 262160 | tf_op jit(solution)/shard_map/psum | solution.py:84
  348.1 1.1 fusion.524
  350.1 4.9 %all_gather.3 = f32[4,8192]{1,0:T(4,128)S(1)} all-gather(f32[4,4096]{1,0:T(4,128)S(1)} %broadcast_divide_fusion), channel_id=1, replica_groups=mesh['groups'=2,'space'=4,'date'=2,'band'=2] {'date'}, dimensions={1}, use_global_device_ids=true | all-gather | bytes 196608 | tf_op jit(solution)/shard_map/all_gather | solution.py:141
  (233 shorter events, 24.2 us)
Async XLA Ops:
  6.5 151.3 %copy-start = (f32[1,128,128]{2,1,0:T(8,128)S(1)}, f32[1,128,128]{2,1,0:T(8,128)}, u32[]{:S(2)}) copy-start(f32[1,128,128]{2,1,0:T(8,128)} %param.15) | copy-start | bytes 196612
  7.9 16.5 %collective-permute-start = (f32[8,4,16,256]{3,2,0,1:T(8,128)S(1)}, f32[8,4,16,256]{3,2,0,1:T(8,128)S(1)}, u32[]{:S(2)}, u32[]{:S(2)}) collective-permute-start(f32[8,4,16,256]{3,2,0,1:T(8,128)S(1)} %get-tuple-element.111), channel_id=1, source_target_pairs={{0,4},{4,8},{8,12},{1,5},{5,9},{9,13},{2,6},{6,10},{10,14},{3,7},{... | collective-permute-start | bytes 1572872 | tf_op jit(solution)/shard_map/ppermute | solution.py:20
  12.9 15.3 %collective-permute-start.1 = (f32[8,4,16,256]{3,2,0,1:T(8,128)S(1)}, f32[8,4,16,256]{3,2,0,1:T(8,128)S(1)}, u32[]{:S(2)}, u32[]{:S(2)}) collective-permute-start(f32[8,4,16,256]{3,2,0,1:T(8,128)S(1)} %get-tuple-element.112), channel_id=1, source_target_pairs={{4,0},{8,4},{12,8},{5,1},{9,5},{13,9},{6,2},{10,6},{14,10},{7,3},{... | collective-permute-start | bytes 1572872 | tf_op jit(solution)/shard_map/ppermute | solution.py:23
  15.3 12.8 %copy-start.51 = (f32[32,64]{1,0:T(8,128)}, f32[32,64]{1,0:T(8,128)S(1)}, u32[]{:S(2)}) copy-start(f32[32,64]{1,0:T(8,128)S(1)} %get-tuple-element.130) | copy-start | bytes 24580
  15.4 12.8 %copy-start.53 = (f32[32,64]{1,0:T(8,128)}, f32[32,64]{1,0:T(8,128)S(1)}, u32[]{:S(2)}) copy-start(f32[32,64]{1,0:T(8,128)S(1)} %get-tuple-element.131) | copy-start | bytes 24580
  15.4 12.8 %copy-start.55 = (f32[32,64]{1,0:T(8,128)}, f32[32,64]{1,0:T(8,128)S(1)}, u32[]{:S(2)}) copy-start(f32[32,64]{1,0:T(8,128)S(1)} %get-tuple-element.132) | copy-start | bytes 24580
  15.4 12.8 %copy-start.57 = (f32[32,64]{1,0:T(8,128)}, f32[32,64]{1,0:T(8,128)S(1)}, u32[]{:S(2)}) copy-start(f32[32,64]{1,0:T(8,128)S(1)} %get-tuple-element.133) | copy-start | bytes 24580
  15.4 12.8 %copy-start.59 = (f32[32,64]{1,0:T(8,128)}, f32[32,64]{1,0:T(8,128)S(1)}, u32[]{:S(2)}) copy-start(f32[32,64]{1,0:T(8,128)S(1)} %get-tuple-element.134) | copy-start | bytes 24580
  22.2 34.7 %copy-start.3 = (f32[256,256]{1,0:T(8,128)}, f32[256,256]{1,0:T(8,128)S(1)}, u32[]{:S(2)}) copy-start(f32[256,256]{1,0:T(8,128)S(1)} %get-tuple-element.160) | copy-start | bytes 786436
  22.3 34.7 %copy-start.4 = (f32[256,256]{1,0:T(8,128)}, f32[256,256]{1,0:T(8,128)S(1)}, u32[]{:S(2)}) copy-start(f32[256,256]{1,0:T(8,128)S(1)} %get-tuple-element.161) | copy-start | bytes 786436
  22.3 34.7 %copy-start.5 = (f32[256,256]{1,0:T(8,128)}, f32[256,256]{1,0:T(8,128)S(1)}, u32[]{:S(2)}) copy-start(f32[256,256]{1,0:T(8,128)S(1)} %get-tuple-element.162) | copy-start | bytes 786436
  22.3 34.6 %copy-start.6 = (f32[256,256]{1,0:T(8,128)}, f32[256,256]{1,0:T(8,128)S(1)}, u32[]{:S(2)}) copy-start(f32[256,256]{1,0:T(8,128)S(1)} %get-tuple-element.163) | copy-start | bytes 786436
  35.6 13.5 %collective-permute-start.2 = (f32[8,4,16,256]{3,2,0,1:T(8,128)S(1)}, f32[8,4,16,256]{3,2,0,1:T(8,128)}, u32[]{:S(2)}, u32[]{:S(2)}) collective-permute-start(f32[8,4,16,256]{3,2,0,1:T(8,128)S(1)} %get-tuple-element.109), channel_id=1, source_target_pairs={{0,4},{4,8},{8,12},{1,5},{5,9},{9,13},{2,6},{6,10},{10,14},{3,7},{... | collective-permute-start | bytes 1572872 | tf_op jit(solution)/shard_map/ppermute | solution.py:20
  39.9 14.2 %collective-permute-start.3 = (f32[8,4,16,256]{3,2,0,1:T(8,128)S(1)}, f32[8,4,16,256]{3,2,0,1:T(8,128)}, u32[]{:S(2)}, u32[]{:S(2)}) collective-permute-start(f32[8,4,16,256]{3,2,0,1:T(8,128)S(1)} %get-tuple-element.110), channel_id=1, source_target_pairs={{4,0},{8,4},{12,8},{5,1},{9,5},{13,9},{6,2},{10,6},{14,10},{7,3},{... | collective-permute-start | bytes 1572872 | tf_op jit(solution)/shard_map/ppermute | solution.py:23
  41.5 15.5 %copy-start.8 = (f32[256,256]{1,0:T(8,128)S(1)}, f32[256,256]{1,0:T(8,128)}, u32[]{:S(2)}) copy-start(f32[256,256]{1,0:T(8,128)} %copy-done.7) | copy-start | bytes 786436
  41.5 15.5 %copy-start.10 = (f32[256,256]{1,0:T(8,128)S(1)}, f32[256,256]{1,0:T(8,128)}, u32[]{:S(2)}) copy-start(f32[256,256]{1,0:T(8,128)} %copy-done.9) | copy-start | bytes 786436
  41.5 15.5 %copy-start.12 = (f32[256,256]{1,0:T(8,128)S(1)}, f32[256,256]{1,0:T(8,128)}, u32[]{:S(2)}) copy-start(f32[256,256]{1,0:T(8,128)} %copy-done.11) | copy-start | bytes 786436
  41.5 15.5 %copy-start.14 = (f32[256,256]{1,0:T(8,128)S(1)}, f32[256,256]{1,0:T(8,128)}, u32[]{:S(2)}) copy-start(f32[256,256]{1,0:T(8,128)} %copy-done.13) | copy-start | bytes 786436
  41.5 15.5 %copy-start.16 = (f32[256,256]{1,0:T(8,128)S(1)}, f32[256,256]{1,0:T(8,128)}, u32[]{:S(2)}) copy-start(f32[256,256]{1,0:T(8,128)} %copy-done.15) | copy-start | bytes 786436
  41.5 15.5 %copy-start.18 = (f32[256,256]{1,0:T(8,128)S(1)}, f32[256,256]{1,0:T(8,128)}, u32[]{:S(2)}) copy-start(f32[256,256]{1,0:T(8,128)} %copy-done.17) | copy-start | bytes 786436
  41.5 15.5 %copy-start.20 = (f32[256,256]{1,0:T(8,128)S(1)}, f32[256,256]{1,0:T(8,128)}, u32[]{:S(2)}) copy-start(f32[256,256]{1,0:T(8,128)} %copy-done.19) | copy-start | bytes 786436
  41.5 15.5 %copy-start.22 = (f32[256,256]{1,0:T(8,128)S(1)}, f32[256,256]{1,0:T(8,128)}, u32[]{:S(2)}) copy-start(f32[256,256]{1,0:T(8,128)} %copy-done.21) | copy-start | bytes 786436
  41.6 15.5 %copy-start.24 = (f32[256,256]{1,0:T(8,128)S(1)}, f32[256,256]{1,0:T(8,128)}, u32[]{:S(2)}) copy-start(f32[256,256]{1,0:T(8,128)} %copy-done.23) | copy-start | bytes 786436
  41.6 15.5 %copy-start.26 = (f32[256,256]{1,0:T(8,128)S(1)}, f32[256,256]{1,0:T(8,128)}, u32[]{:S(2)}) copy-start(f32[256,256]{1,0:T(8,128)} %copy-done.25) | copy-start | bytes 786436
  41.6 15.5 %copy-start.28 = (f32[256,256]{1,0:T(8,128)S(1)}, f32[256,256]{1,0:T(8,128)}, u32[]{:S(2)}) copy-start(f32[256,256]{1,0:T(8,128)} %copy-done.27) | copy-start | bytes 786436
  41.6 15.5 %copy-start.30 = (f32[256,256]{1,0:T(8,128)S(1)}, f32[256,256]{1,0:T(8,128)}, u32[]{:S(2)}) copy-start(f32[256,256]{1,0:T(8,128)} %copy-done.29) | copy-start | bytes 786436
  41.6 15.5 %copy-start.32 = (f32[256,256]{1,0:T(8,128)S(1)}, f32[256,256]{1,0:T(8,128)}, u32[]{:S(2)}) copy-start(f32[256,256]{1,0:T(8,128)} %copy-done.31) | copy-start | bytes 786436
  41.6 15.5 %copy-start.34 = (f32[256,256]{1,0:T(8,128)S(1)}, f32[256,256]{1,0:T(8,128)}, u32[]{:S(2)}) copy-start(f32[256,256]{1,0:T(8,128)} %copy-done.33) | copy-start | bytes 786436
  41.6 15.5 %copy-start.36 = (f32[256,256]{1,0:T(8,128)S(1)}, f32[256,256]{1,0:T(8,128)}, u32[]{:S(2)}) copy-start(f32[256,256]{1,0:T(8,128)} %copy-done.35) | copy-start | bytes 786436
  63.4 16.0 %copy-start.52 = (f32[32,64]{1,0:T(8,128)S(1)}, f32[32,64]{1,0:T(8,128)}, u32[]{:S(2)}) copy-start(f32[32,64]{1,0:T(8,128)} %copy-done.51) | copy-start | bytes 24580
  63.4 16.0 %copy-start.54 = (f32[32,64]{1,0:T(8,128)S(1)}, f32[32,64]{1,0:T(8,128)}, u32[]{:S(2)}) copy-start(f32[32,64]{1,0:T(8,128)} %copy-done.53) | copy-start | bytes 24580
  63.4 16.0 %copy-start.56 = (f32[32,64]{1,0:T(8,128)S(1)}, f32[32,64]{1,0:T(8,128)}, u32[]{:S(2)}) copy-start(f32[32,64]{1,0:T(8,128)} %copy-done.55) | copy-start | bytes 24580
  63.4 16.0 %copy-start.58 = (f32[32,64]{1,0:T(8,128)S(1)}, f32[32,64]{1,0:T(8,128)}, u32[]{:S(2)}) copy-start(f32[32,64]{1,0:T(8,128)} %copy-done.57) | copy-start | bytes 24580
  63.4 16.0 %copy-start.60 = (f32[32,64]{1,0:T(8,128)S(1)}, f32[32,64]{1,0:T(8,128)}, u32[]{:S(2)}) copy-start(f32[32,64]{1,0:T(8,128)} %copy-done.59) | copy-start | bytes 24580
  63.4 16.0 %copy-start.62 = (f32[32,64]{1,0:T(8,128)S(1)}, f32[32,64]{1,0:T(8,128)}, u32[]{:S(2)}) copy-start(f32[32,64]{1,0:T(8,128)} %copy-done.61) | copy-start | bytes 24580
  63.4 16.0 %copy-start.64 = (f32[32,64]{1,0:T(8,128)S(1)}, f32[32,64]{1,0:T(8,128)}, u32[]{:S(2)}) copy-start(f32[32,64]{1,0:T(8,128)} %copy-done.63) | copy-start | bytes 24580
  63.5 11.6 %collective-permute-start.4 = (f32[8,4,16,256]{3,2,0,1:T(8,128)S(1)}, f32[8,4,16,256]{3,2,0,1:T(8,128)S(1)}, u32[]{:S(2)}, u32[]{:S(2)}) collective-permute-start(f32[8,4,16,256]{3,2,0,1:T(8,128)S(1)} %get-tuple-element.107), channel_id=1, source_target_pairs={{0,4},{4,8},{8,12},{1,5},{5,9},{9,13},{2,6},{6,10},{10,14},{3,7},{... | collective-permute-start | bytes 1572872 | tf_op jit(solution)/shard_map/ppermute | solution.py:20
  66.2 13.1 %collective-permute-start.5 = (f32[8,4,16,256]{3,2,0,1:T(8,128)S(1)}, f32[8,4,16,256]{3,2,0,1:T(8,128)}, u32[]{:S(2)}, u32[]{:S(2)}) collective-permute-start(f32[8,4,16,256]{3,2,0,1:T(8,128)S(1)} %get-tuple-element.108), channel_id=1, source_target_pairs={{4,0},{8,4},{12,8},{5,1},{9,5},{13,9},{6,2},{10,6},{14,10},{7,3},{... | collective-permute-start | bytes 1572872 | tf_op jit(solution)/shard_map/ppermute | solution.py:23
  68.4 25.1 %all-to-all-start.2 = ((f32[4,1,8]{2,1,0:T(1,128)}), f32[4,1,8]{2,1,0:T(1,128)S(1)}, u32[]{:S(2)}, u32[]{:S(2)}) async-start(f32[4,1,8]{2,1,0:T(1,128)} %bitcast.43), calls=%async_computation.2 | async-start | bytes 4096 | tf_op jit(solution)/shard_map/all_to_all | solution.py:122
  93.5 60.5 %copy-start.65 = (f32[1,4,4]{2,1,0:T(4,128)S(1)}, f32[1,4,4]{2,1,0:T(4,128)}, u32[]{:S(2)}) copy-start(f32[1,4,4]{2,1,0:T(4,128)} %param.14) | copy-start | bytes 196
  93.5 50.9 %all-to-all-start.1 = ((f32[4,8,8,4,4,128]{5,1,4,3,2,0:T(8,128)}), f32[4,8,8,4,4,128]{5,1,4,3,2,0:T(8,128)S(1)}, u32[]{:S(2)}, u32[]{:S(2)}) async-start(f32[4,8,8,4,4,128]{5,1,4,3,2,0:T(8,128)} %fusion.56), calls=%async_computation.1 | async-start | bytes 4194304 | tf_op jit(solution)/shard_map/all_to_all | solution.py:121
  145.0 53.7 %all-to-all-start = ((f32[8,1,2]{0,1,2:T(1,128)}), f32[8,1,2]{0,1,2:T(1,128)S(1)}, u32[]{:S(2)}, u32[]{:S(2)}) async-start(f32[8,1,2]{0,1,2:T(1,128)} %broadcast_in_dim.5), calls=%async_computation | async-start | bytes 2048 | tf_op jit(solution)/shard_map/all_to_all | solution.py:138
  198.7 14.3 %all-to-all-start.3 = ((f32[2,1,131072]{2,1,0:T(1,128)}), f32[2,1,131072]{2,1,0:T(1,128)S(1)}, u32[]{:S(2)}, u32[]{:S(2)}) async-start(f32[2,1,131072]{2,1,0:T(1,128)} %reshape.1121), calls=%async_computation.3 | async-start | bytes 2097152 | tf_op jit(solution)/shard_map/all_to_all | solution.py:137
  202.3 76.5 %all-reduce.5.cloned.1.call-start = ((), (), s32[]{:S(2)}) async-start(), calls=%async_computation.4 | async-start | bytes 524288 | tf_op jit(solution)/shard_map/psum | solution.py:84
  259.5 42.3 %all-reduce.7.cloned.1.call-start = ((), (), s32[]{:S(2)}) async-start(), calls=%async_computation.5 | async-start | bytes 524288 | tf_op jit(solution)/shard_map/psum | solution.py:84
  282.2 42.7 %all-reduce.9.cloned.1.call-start = ((), (), s32[]{:S(2)}) async-start(), calls=%async_computation.6 | async-start | bytes 524288 | tf_op jit(solution)/shard_map/psum | solution.py:84
  305.4 42.7 %all-reduce.11.cloned.1.call-start = ((), (), s32[]{:S(2)}) async-start(), calls=%async_computation.7 | async-start | bytes 524288 | tf_op jit(solution)/shard_map/psum | solution.py:84
  326.9 28.7 %copy-start.1 = (f32[1,128,128]{2,1,0:T(8,128)S(1)}, f32[1,128,128]{2,1,0:T(8,128)}, u32[]{:S(2)}) copy-start(f32[1,128,128]{2,1,0:T(8,128)} %param.15) | copy-start | bytes 196612
  (36 other events, 279.9 us)
Sparse Core Ops, SparseCore 0:
  259.7 19.0 all-reduce.4
  282.4 19.4 all-reduce.6
  305.5 19.4 all-reduce.8
  328.6 19.4 all-reduce.10
where the time goes:
time: 370 us; the launch traced here: 363 us
  waiting for transfers between devices  108 us (29%)
  local copies, waits for them, and re-layouts  89.1 us (24%)
  blocking collectives  50.7 us (14%)
  starting transfers between devices  37.2 us (10%)
  matrix products  36.9 us (10%)
  other arithmetic  24.6 us (7%)
  between operations  15.8 us (4%)
    psum x4, waiting for transfers between devices, band_total(): return lax.psum(squares, 'band')  77.4 us
    unnamed x143, local copies, waits for them, and re-layouts  55.2 us
    psum x1, blocking collectives, local(): count_sum = lax.psum(count_part, ('space', 'date'))  45.7 us
    dot_general x3, matrix products, correct_strip(): jnp.einsum('tbrj,bcj->tbrc', row_pass, column_matrix, precision=highest)  18 us
    all_to_all x2, local copies, waits for them, and re-layouts, local(): lax.all_to_all(stacked, 'date', split_axis=2, concat_axis=0, tiled=True)  13.7 us
    ppermute x3, waiting for transfers between devices, padded_2(): lax.ppermute(lax.slice_in_dim(block, 0, width, axis=dim), axis, backward)  13 us
    ppermute x3, starting transfers between devices, padded_2(): lax.ppermute(lax.slice_in_dim(block, block.shape[dim] - width, None, axis...  12 us
    all_to_all x1, waiting for transfers between devices, local(): lax.all_to_all(stacked, 'date', split_axis=2, concat_axis=0, tiled=True)  9.74 us
  transfers between devices with their start and end apart: 14, of which 10 were waited for; matrix products, arithmetic and copies ran while one was open for 20% of the time, Pallas kernels for 0%

commit v1 on v0

v1 whole, which is shorter than its diff:
```python
import functools

import jax
import jax.numpy as jnp
from jax import lax
from jax.experimental import pallas as pl
from jax.experimental.pallas import tpu as pltpu
from jax.sharding import PartitionSpec as P

BROWS = 4
BCOLS = 128
ITERS = 4
LANES = 128

smooth_sq = 0.01
f32 = jnp.float32
bf16 = jnp.bfloat16


def split(x):
    high = x.astype(bf16)
    return high, (x - high.astype(f32)).astype(bf16)


def mm(a, b):
    return jnp.dot(a, b, preferred_element_type=f32)


def toeplitz_kernel(row_ref, col_ref, rh_ref, rl_ref, ch_ref, cl_ref):
    count, wide = row_ref.shape
    for src, high_ref, low_ref in ((row_ref, rh_ref, rl_ref), (col_ref, ch_ref, cl_ref)):
        size = high_ref.shape[1]
        for k in range(count):
            line = jnp.broadcast_to(src[k : k + 1, :], (size, wide))
            band = pltpu.roll(line, 0, 1, stride=1, stride_axis=0)[:, :size]
            high, low = split(band)
            high_ref[k] = high
            low_ref[k] = low


def wrapped(taps, wide):
    taps_count = taps.shape[-1]
    half = taps_count // 2
    pad = jnp.zeros(taps.shape[:-1] + (wide - taps_count,), f32)
    return jnp.concatenate([taps[..., half:], pad, taps[..., :half]], axis=-1)


def correct_kernel(
    gain_ref, x_ref, rh_ref, rl_ref, ch_ref, cl_ref, base_ref, rows_ref, out_ref, *, passes, bands
):
    spaces, per, strip, width = x_ref.shape
    rows = spaces * strip
    halves = width // BCOLS
    done = [None] * per
    for band in range(bands):
        members = range(band, per, bands)
        images = [
            jnp.concatenate([x_ref[s, i] for s in range(spaces)], axis=0) for i in members
        ]
        for step in range(passes):
            k = step * bands + band
            rh, rl, ch, cl = rh_ref[k], rl_ref[k], ch_ref[k], cl_ref[k]
            gain = gain_ref[k]
            parts = []
            for image in images:
                xh, xl = split(image)
                parts.append(mm(rh, xh) + (mm(rl, xh) + mm(rh, xl)))
            stacked = jnp.concatenate(parts, axis=0)
            yh, yl = split(stacked)
            blurred = mm(yh, ch) + (mm(yl, ch) + mm(yh, cl))
            images = [
                gain * image - blurred[q * rows : (q + 1) * rows]
                for q, image in enumerate(images)
            ]
        for i, image in zip(members, images):
            done[i] = jnp.concatenate(
                [image[:, h * BCOLS : (h + 1) * BCOLS] for h in range(halves)], axis=0
            )
    line = lax.broadcasted_iota(jnp.int32, (out_ref.shape[0] * out_ref.shape[2], rows * halves), 0)
    first = line - base_ref[...]
    placer = jnp.zeros(line.shape, f32)
    for i in range(BROWS):
        placer = jnp.where(first == i, rows_ref[i : i + 1, :], placer)
    ah, al = split(placer)
    share = out_ref.shape[2]
    for i in range(per):
        zh, zl = split(done[i])
        laid = mm(ah, zh) + (mm(al, zh) + mm(ah, zl))
        for d in range(out_ref.shape[0]):
            out_ref[d, i] = laid[d * share : (d + 1) * share]


def median_kernel(weight_ref, y_ref, cols_ref, out_ref, full_ref, *, spaces, dates, cores, bands, local_dates):
    sources, per, share, width = y_ref.shape
    kh, kl = split(cols_ref[...])
    for s in range(sources):
        block = y_ref[s].reshape(per * share, width)
        bh, bl = split(block)
        full = mm(bh, kh) + (mm(bl, kh) + mm(bh, kl))
        full_ref[s] = full.reshape(per, share, width)
    total_bands = cores * bands
    where = [[None] * total_bands for _ in range(dates * local_dates)]
    for z in range(spaces):
        for x in range(dates):
            for c in range(cores):
                for i in range(per):
                    t, b = divmod(z * per + i, bands)
                    where[x * local_dates + t][c * bands + b] = ((z * dates + x) * cores + c, i)
    tile = min(share, 8)
    for start in range(0, share, tile):
        rows = pl.ds(start, tile)

        def load(t):
            return [full_ref[s, i, rows, :] for s, i in where[t]]

        number = [jnp.zeros((tile, width), f32)] * total_bands
        weight_sum = f32(0)
        for t, _ in enumerate(where):
            w = weight_ref[t]
            weight_sum = weight_sum + w
            number = [n + w * v for n, v in zip(number, load(t))]
        estimate = [n / weight_sum for n in number]
        for _ in range(ITERS):
            number = [jnp.zeros((tile, width), f32)] * total_bands
            below = jnp.zeros((tile, width), f32)
            for t, _ in enumerate(where):
                values = load(t)
                square = jnp.full((tile, width), smooth_sq, f32)
                for v, e in zip(values, estimate):
                    d = v - e
                    square = square + d * d
                scaled = weight_ref[t] / jnp.sqrt(square)
                below = below + scaled
                number = [n + scaled * v for n, v in zip(number, values)]
            estimate = [n / below for n in number]
        for x in range(dates):
            for b in range(total_bands):
                out_ref[x * cores + b // bands, b % bands, rows, :] = estimate[b]


def vmem(count):
    return [pl.BlockSpec(memory_space=pltpu.VMEM)] * count


def smem():
    return pl.BlockSpec(memory_space=pltpu.SMEM)


def local(
    reflect, kernels, strength, destinations, offsets, counts, resample_rows, resample_columns
):
    spaces, dates, cores = (lax.axis_size(a) for a in ("space", "date", "band"))
    local_dates, bands, strip, width = reflect.shape
    passes = kernels.shape[0]
    blocks = offsets.shape[0]
    rows = spaces * strip
    halves = width // BCOLS
    tile_rows = blocks * BROWS
    sources = spaces * dates * cores
    share = tile_rows // (dates * cores)
    per = local_dates * bands // spaces

    images = reflect.reshape(local_dates * bands, strip, width)
    whole = lax.all_to_all(images, "space", split_axis=0, concat_axis=0, tiled=True)

    packed = jnp.concatenate(
        [
            destinations[:, 0].astype(f32),
            offsets.astype(f32),
            resample_rows.reshape(-1),
            counts[:, 0].astype(f32),
        ]
    )
    used = packed.shape[0]
    lanes = -(-used // LANES) * LANES
    packed = jnp.pad(packed, (0, lanes - used))
    spread = jnp.broadcast_to(packed[None, None, :], (spaces * dates, 1, lanes))
    small = lax.all_to_all(spread, ("space", "date"), split_axis=0, concat_axis=0, tiled=True)
    small = small.reshape(spaces, dates, lanes)

    here = bands if per % bands == 0 else per
    if here != bands:
        first_band = (lax.axis_index("space") * per) % bands
        kernels = lax.dynamic_slice_in_dim(kernels, first_band, here, axis=1)
        strength = lax.dynamic_slice_in_dim(strength, first_band, here, axis=1)
    taps = kernels / jnp.sum(kernels, axis=2, keepdims=True)
    wide = max(rows, width) + LANES
    row_taps = wrapped(taps * strength[:, :, None], wide).reshape(passes * here, wide)
    column_taps = wrapped(taps[:, :, ::-1], wide).reshape(passes * here, wide)
    gains = (1.0 + strength).reshape(-1)
    count = passes * here
    rh, rl, ch, cl = pl.pallas_call(
        toeplitz_kernel,
        out_shape=[jax.ShapeDtypeStruct((count, rows, rows), bf16)] * 2
        + [jax.ShapeDtypeStruct((count, width, width), bf16)] * 2,
        in_specs=vmem(2),
        out_specs=vmem(4),
        name="toeplitz",
    )(row_taps, column_taps)

    of_strip = small[:, 0, :]
    targets = of_strip[:, :blocks]
    starts = of_strip[:, blocks : 2 * blocks]
    matrices = of_strip[:, 2 * blocks : 2 * blocks + BROWS * BROWS].reshape(spaces, BROWS, BROWS)

    def by_row(table):
        table = table.reshape(spaces, strip // BROWS, halves).transpose(2, 0, 1)
        table = jnp.broadcast_to(table[..., None], table.shape + (BROWS,))
        return table.reshape(1, halves * rows)

    base = by_row(targets * tile_rows + starts).astype(jnp.int32)
    target_of = by_row(targets)
    repeats = halves * rows // BROWS
    entries = jnp.zeros((BROWS, halves * rows), f32)
    for g in range(spaces):
        entries = entries + jnp.where(target_of == g, jnp.tile(matrices[g], (1, repeats)), 0.0)

    laid = pl.pallas_call(
        functools.partial(correct_kernel, passes=passes, bands=here),
        out_shape=jax.ShapeDtypeStruct((sources, per, share, BCOLS), f32),
        in_specs=[smem()] + vmem(7),
        out_specs=pl.BlockSpec(memory_space=pltpu.VMEM),
        name="correct",
    )(gains, whole.reshape(spaces, per, strip, width), rh, rl, ch, cl, base, entries)

    pixels = lax.all_to_all(
        laid, ("space", "date", "band"), split_axis=0, concat_axis=0, tiled=True
    )

    counted = small[:, :, 2 * blocks + BROWS * BROWS :][:, :, :local_dates]
    mean_count = jnp.sum(counted) / (spaces * dates * local_dates)
    own = lax.dynamic_slice_in_dim(counted, lax.axis_index("space"), 1, axis=0).reshape(-1)
    weights = own / (own + mean_count)

    parts = pl.pallas_call(
        functools.partial(
            median_kernel,
            spaces=spaces,
            dates=dates,
            cores=cores,
            bands=bands,
            local_dates=local_dates,
        ),
        out_shape=jax.ShapeDtypeStruct((dates * cores, bands, share, BCOLS), f32),
        in_specs=[smem()] + vmem(2),
        out_specs=pl.BlockSpec(memory_space=pltpu.VMEM),
        scratch_shapes=[pltpu.VMEM((sources, per, share, BCOLS), f32)],
        name="median",
    )(weights, pixels, resample_columns[0])

    shares = lax.all_to_all(parts, ("date", "band"), split_axis=0, concat_axis=0, tiled=True)
    return shares.transpose(1, 0, 2, 3).reshape(bands, tile_rows, BCOLS)


def solution(mesh):
    in_specs = (
        P("date", "band", ("groups", "space"), None),
        P(None, "band", None),
        P(None, "band"),
        P(("groups", "space"), None),
        P(("groups", "space")),
        P("date", ("groups", "space")),
        P(("groups", "space"), None, None),
        P(("groups", "space"), None, None),
    )
    out_specs = P("band", ("groups", "space"), None)
    return jax.shard_map(local, mesh=mesh, in_specs=in_specs, out_specs=out_specs, check_vma=False)
```

time: 370 us -> 96.3 us (0.26); the launches traced: 363 us -> 95.2 us
  local copies, waits for them, and re-layouts: 89.1 us -> 9.24 us
  waiting for transfers between devices: 108 us -> 35.1 us
  matrix products: 36.9 us -> 0 us
  starting transfers between devices: 37.2 us -> 7.17 us
  blocking collectives: 50.7 us -> 22 us
  other arithmetic: 24.6 us -> 4.29 us
  Pallas kernels: 0 us -> 16.7 us
  between operations: 15.8 us -> 0.76 us
    psum x4 -> x0, waiting for transfers between devices: 77.4 us -> none  [band_total(): return lax.psum(squares, 'band')]
    unnamed x143 -> x8, local copies, waits for them, and re-layouts: 55.2 us -> 1.97 us
    psum x1 -> x0, blocking collectives: 45.7 us -> none  [local(): count_sum = lax.psum(count_part, ('space', 'date'))]
    dot_general x11 -> x0, matrix products: 36.9 us -> none  [the longest x3 18 us: correct_strip(): jnp.einsum('tbrj,bcj->tbrc', row_pass, column_matrix, precision=highest)]
    all_to_all x4 -> x2, waiting for transfers between devices: 9.75 us -> 35.1 us  [the longest x1 20.8 us: local(): lax.all_to_all(laid, ('space', 'date', 'band'), split_axis=0, concat_axis...]
    all_to_all x0 -> x2, blocking collectives: none -> 22 us  [the longest x1 13.6 us: local(): lax.all_to_all(spread, ('space', 'date'), split_axis=0, concat_axis=0, ti...]
    ppermute x6 -> x0, waiting for transfers between devices: 21.1 us -> none  [the longest x3 13 us: padded_2(): lax.ppermute(lax.slice_in_dim(block, 0, width, axis=dim), axis, backward)]
    pallas_call x0 -> x3, Pallas kernels: none -> 16.7 us  [the longest x1 9.74 us: local(): pl.pallas_call(functools.partial(correct_kernel, passes=passes, bands=her...]
  transfers between devices with their start and end apart: 14 -> 2, of which waited for: 10 -> 2; matrix products, arithmetic and copies ran while one was open for 20% -> 8% of each run, Pallas kernels for 0% -> 4%
where the time goes in v1:
time: 96.3 us; the launch traced here: 95.2 us
  waiting for transfers between devices  35.1 us (36%)
  blocking collectives  22 us (23%)
  Pallas kernels  16.7 us (17%)
  local copies, waits for them, and re-layouts  9.24 us (10%)
  starting transfers between devices  7.17 us (7%)
  other arithmetic  4.29 us (4%)
    all_to_all x1, waiting for transfers between devices, local(): lax.all_to_all(laid, ('space', 'date', 'band'), split_axis=0, concat_axis...  20.8 us
    all_to_all x1, waiting for transfers between devices, local(): lax.all_to_all(images, 'space', split_axis=0, concat_axis=0, tiled=True)  14.3 us
    all_to_all x1, blocking collectives, local(): lax.all_to_all(spread, ('space', 'date'), split_axis=0, concat_axis=0, ti...  13.6 us
    pallas_call x1, Pallas kernels, local(): pl.pallas_call(functools.partial(correct_kernel, passes=passes, bands=her...  9.74 us
    all_to_all x1, blocking collectives, local(): lax.all_to_all(parts, ('date', 'band'), split_axis=0, concat_axis=0, tile...  8.4 us
    all_to_all x1, starting transfers between devices, local(): lax.all_to_all(laid, ('space', 'date', 'band'), split_axis=0, concat_axis...  3.65 us
    all_to_all x1, starting transfers between devices, local(): lax.all_to_all(images, 'space', split_axis=0, concat_axis=0, tiled=True)  3.52 us
    pallas_call x1, Pallas kernels, local(): pl.pallas_call(toeplitz_kernel, out_shape=[jax.ShapeDtypeStruct((count, r...  3.5 us
  transfers between devices with their start and end apart: 2, of which 2 were waited for; matrix products, arithmetic and copies ran while one was open for 8% of the time, Pallas kernels for 4%

profile of v1, /device:TPU:0, one launch (start us, length us, event | category | flops | bytes accessed | tf_op | source)
XLA Modules:
  0.0 95.2 jit_solution(11682667283129305280)
XLA Ops:
  0.0 0.7 convert_bitcast_fusion.1
  0.7 0.7 convert_element_type.28
  1.3 0.7 convert_bitcast_fusion
  2.0 0.8 reshape.123
  2.9 13.6 %all_to_all.20 = f32[8,1,128]{2,1,0:T(1,128)S(1)} all-to-all(f32[8,1,128]{2,1,0:T(1,128)S(1)} %broadcast_in_dim.56), channel_id=1, replica_groups=mesh['groups'=2,'space'=4,'date'=2,'band'=2] {'space','date'}, dimensions={0} | all-to-all | bytes 8192 | tf_op jit(solution)/shard_map/all_to_all | solution.py:178
  16.4 3.5 %all-to-all-start.1 = ((f32[32,32,256]{2,1,0:T(8,128)}), f32[32,32,256]{2,1,0:T(8,128)S(1)}, u32[]{:S(2)}, u32[]{:S(2)}) async-start(f32[32,32,256]{2,1,0:T(8,128)} %bitcast.31), calls=%async_computation.1 | async-start | bytes 2097152 | tf_op jit(solution)/shard_map/all_to_all | solution.py:164
  20.0 0.6 reshape.126.gain_ref
  20.6 0.1 reduce_sum.19
  20.8 0.1 slice.57
  21.0 0.1 slice.59
  21.2 0.1 pad_maximum_fusion.1
  21.3 0.6 reshape.130.col_ref
  21.9 0.6 reshape.129.row_ref
  22.5 3.5 %toeplitz.1 = (bf16[12,128,128]{2,1,0:T(8,128)(2,1)}, bf16[12,128,128]{2,1,0:T(8,128)(2,1)}, bf16[12,256,256]{2,1,0:T(8,128)(2,1)}, bf16[12,256,256]{2,1,0:T(8,128)(2,1)}) custom-call(f32[12,384]{1,0:T(8,128)} %reshape.129.row_ref, f32[12,384]{1,0:T(8,128)} %reshape.130.col_ref), custom_call_target="tpu_custom_call" | custom-call | tf_op jit(solution)/shard_map/toeplitz/pallas_call | solution.py:192
  26.0 0.1 slice_reduce_fusion.3
  26.4 0.1 eq.86
  26.5 0.1 copy.27
  26.6 0.1 eq.91
  26.7 0.1 copy.28
  26.8 0.1 eq.96
  26.9 0.1 copy.29
  27.0 0.1 eq.101
  27.1 0.1 copy.30
  27.3 0.1 copy.25
  27.4 0.1 copy.26
  27.5 0.1 broadcast_in_dim.65
  27.6 0.1 eq.103
  27.8 0.1 eq.98
  28.0 0.1 eq.93
  28.2 0.1 eq.88
  28.4 0.7 convert_element_type.34.base_ref
  29.1 0.1 tile.45
  29.2 0.1 tile.48
  29.3 0.1 tile.51
  29.5 0.1 tile.42
  29.6 0.6 select_add_fusion.rows_ref
  30.2 14.3 %all-to-all-done.1 = f32[32,32,256]{2,1,0:T(8,128)S(1)} async-done(((f32[32,32,256]{2,1,0:T(8,128)}), f32[32,32,256]{2,1,0:T(8,128)S(1)}, u32[]{:S(2)}, u32[]{:S(2)}) %all-to-all-start.1) | async-done | bytes 1048608 | tf_op jit(solution)/shard_map/all_to_all | solution.py:164
  44.5 1.0 %copy-done.1 = f32[32,32,256]{2,1,0:T(8,128)} copy-done((f32[32,32,256]{2,1,0:T(8,128)}, f32[32,32,256]{2,1,0:T(8,128)S(1)}, u32[]{:S(2)}) %copy-start.1) | copy-done | bytes 1048600
  45.5 9.7 %correct.1 = f32[16,8,16,128]{3,2,1,0:T(8,128)} custom-call(f32[12]{0:T(128)} %reshape.126.gain_ref, f32[4,8,32,256]{3,2,1,0:T(8,128)} %bitcast.30, bf16[12,128,128]{2,1,0:T(8,128)(2,1)} %get-tuple-element.9.rh_ref, bf16[12,128,128]{2,1,0:T(8,128)(2,1)} %get-tuple-element.10.rl_ref, bf16[12,256,256]{2,1,0:T(8,128)(2,1)} %get-tuple-element.11.ch_ref, ...), custom_call_target="tpu_custom_call" | custom-call | tf_op jit(solution)/shard_map/correct/pallas_call | solution.py:218
  55.2 3.7 %all-to-all-start.2 = ((f32[16,8,16,128]{3,2,1,0:T(8,128)}), f32[16,8,16,128]{3,2,1,0:T(8,128)S(1)}, u32[]{:S(2)}, u32[]{:S(2)}) async-start(f32[16,8,16,128]{3,2,1,0:T(8,128)} %correct.1), calls=%async_computation.2 | async-start | bytes 2097152 | tf_op jit(solution)/shard_map/all_to_all | solution.py:226
  58.9 0.7 slice_reduce_fusion.4
  59.5 0.1 reshape.125
  60.3 0.6 add_divide_fusion.weight_ref
  60.9 20.8 %all-to-all-done.2.y_ref = f32[16,8,16,128]{3,2,1,0:T(8,128)S(1)} async-done(((f32[16,8,16,128]{3,2,1,0:T(8,128)}), f32[16,8,16,128]{3,2,1,0:T(8,128)S(1)}, u32[]{:S(2)}, u32[]{:S(2)}) %all-to-all-start.2) | async-done | bytes 1048608 | tf_op jit(solution)/shard_map/all_to_all | solution.py:226
  81.7 1.0 %copy-done = f32[16,8,16,128]{3,2,1,0:T(8,128)} copy-done((f32[16,8,16,128]{3,2,1,0:T(8,128)}, f32[16,8,16,128]{3,2,1,0:T(8,128)S(1)}, u32[]{:S(2)}) %copy-start) | copy-done | bytes 1048600
  82.7 3.4 %median.1 = f32[4,4,16,128]{3,2,1,0:T(8,128)} custom-call(f32[16]{0:T(128)} %add_divide_fusion.weight_ref, f32[16,8,16,128]{3,2,1,0:T(8,128)} %copy-done, f32[128,128]{1,0:T(8,128)} %bitcast.33), custom_call_target="tpu_custom_call" | custom-call | tf_op jit(solution)/shard_map/median/pallas_call | solution.py:235
  86.1 8.4 %all_to_all.21 = f32[4,4,16,128]{3,2,1,0:T(8,128)S(1)} all-to-all(f32[4,4,16,128]{3,2,1,0:T(8,128)} %median.1), channel_id=1, replica_groups=mesh['groups'=2,'space'=4,'date'=2,'band'=2] {'date','band'}, dimensions={0} | all-to-all | bytes 262144 | tf_op jit(solution)/shard_map/all_to_all | solution.py:251
  94.5 0.7 copy.31
  (30 shorter events, 1.2 us)
Async XLA Ops:
  0.0 19.9 %copy-start.3 = (f32[3,4]{1,0:T(4,128)S(1)}, f32[3,4]{1,0:T(4,128)}, u32[]{:S(2)}) copy-start(f32[3,4]{1,0:T(4,128)} %param.10) | copy-start | bytes 148
  0.0 20.6 %copy-start.2 = (f32[3,4,33]{2,1,0:T(4,128)S(1)}, f32[3,4,33]{2,1,0:T(4,128)}, u32[]{:S(2)}) copy-start(f32[3,4,33]{2,1,0:T(4,128)} %param.9) | copy-start | bytes 4756
  16.4 28.1 %all-to-all-start.1 = ((f32[32,32,256]{2,1,0:T(8,128)}), f32[32,32,256]{2,1,0:T(8,128)S(1)}, u32[]{:S(2)}, u32[]{:S(2)}) async-start(f32[32,32,256]{2,1,0:T(8,128)} %bitcast.31), calls=%async_computation.1 | async-start | bytes 2097152 | tf_op jit(solution)/shard_map/all_to_all | solution.py:164
  44.5 1.0 %copy-start.1 = (f32[32,32,256]{2,1,0:T(8,128)}, f32[32,32,256]{2,1,0:T(8,128)S(1)}, u32[]{:S(2)}) copy-start(f32[32,32,256]{2,1,0:T(8,128)S(1)} %all-to-all-done.1) | copy-start | bytes 3145732
  55.2 26.5 %all-to-all-start.2 = ((f32[16,8,16,128]{3,2,1,0:T(8,128)}), f32[16,8,16,128]{3,2,1,0:T(8,128)S(1)}, u32[]{:S(2)}, u32[]{:S(2)}) async-start(f32[16,8,16,128]{3,2,1,0:T(8,128)} %correct.1), calls=%async_computation.2 | async-start | bytes 2097152 | tf_op jit(solution)/shard_map/all_to_all | solution.py:226
  81.7 1.0 %copy-start = (f32[16,8,16,128]{3,2,1,0:T(8,128)}, f32[16,8,16,128]{3,2,1,0:T(8,128)S(1)}, u32[]{:S(2)}) copy-start(f32[16,8,16,128]{3,2,1,0:T(8,128)S(1)} %all-to-all-done.2.y_ref) | copy-start | bytes 3145732
